TPU v7x, 32 devices: a whole 2x2x4 slice. The times are simulated.
32 devices in a mesh: pipe: 2 (over core), node: 8 (over z, x), head: 2 (over y).
Axes of the slice: x: 2, y: 2, z: 4, core: 2. Of those that a mesh axis runs over, the one named last changes fastest.
Arguments:
- feats: bfloat16 [2, 1024, 2048], P(None, 'node', 'head'), may hold values from -20 to 20
- gain: float32 [2, 2048], P('pipe'), may hold values from 0.25 to 1.75
- w_qkv: bfloat16 [2, 3, 2048, 2048], P('pipe', None, 'node', 'head'), may hold values from -0.176776695 to 0.176776695
- w_out: bfloat16 [2, 2048, 2048], P('pipe', 'head', 'node'), may hold values from -1 to 1
- block_mask: int32 [2, 8, 8], replicated, may hold values from 0 to 1, as said below
Outputs:
- layers_out: bfloat16 [2, 2, 1024, 2048], P('pipe', None, 'node', 'head')
Inputs may be any that keep to these rules, and one draw needn't show every extreme that they name: block_mask[m, b, b] = 1; block_mask[m, b, c] is 0 unless c = b or c = b xor 2^k with k one of L - 1, L // 2 and 0, where 2^L = 8.
All inputs are finite; a program needn't handle non-finite values.
Results may differ from a plain program's by a relative error of at most 0.023.
Values may be sent and summed in bfloat16 or wider, within the bound.
A program may use at most 64 MiB of HBM per device.

v0:
```python
import functools
import jax
import jax.numpy as jnp
from jax import lax
from jax.experimental import pallas as pl
from jax.experimental.pallas import tpu as pltpu
from jax.sharding import PartitionSpec as P

HD = 128
MICRO = 2


EPS = 1e-06
NEG = -1e30


def from_partner(block, axis, apart):
    count = lax.axis_size(axis)
    route = []
    for low in range(count):
        high = low | 1 << apart
        if high != low and high < count:
            route += [(low, high), (high, low)]
    return lax.ppermute(block, axis, route)


def from_behind(value, axis, steps):
    count = lax.axis_size(axis)
    first, last = (max(0, -steps), min(count, count - steps))
    return lax.ppermute(value, axis, [(source, source + steps) for source in range(first, last)])


def partial_attend(query, key, value, keep):
    rows = query.shape[0]
    groups = query.shape[1] // HD
    q_heads = query.reshape(rows, groups, HD)
    k_heads = key.reshape(key.shape[0], groups, HD)
    v_heads = value.reshape(value.shape[0], groups, HD)
    scores = jnp.einsum("qhd,khd->hqk", q_heads, k_heads, preferred_element_type=jnp.float32) * (
        1.0 / HD**0.5
    )
    scores = jnp.where(keep[None, None, :], scores, NEG)
    top = jnp.max(scores, axis=-1)
    expo = jnp.where(keep[None, None, :], jnp.exp(scores - top[..., None]), 0.0)
    total = jnp.sum(expo, axis=-1)
    summed = jnp.einsum(
        "hqk,khd->hqd", expo.astype(jnp.bfloat16), v_heads, preferred_element_type=jnp.float32
    )
    return (summed, top, total)


def finish(summed, total):
    out = summed / total[..., None]
    rows = out.shape[1]
    return jnp.transpose(out, (1, 0, 2)).reshape(rows, -1).astype(jnp.bfloat16)


def local_any(feats, gain, w_qkv, w_out, block_mask):
    segment = lax.axis_index("pipe")
    me = lax.axis_index("node")
    width = lax.axis_size("node").bit_length() - 1
    bit_list = [width - 1, width // 2, 0]
    qkv_whole, out_whole = (
        lax.all_gather(w_qkv, "node", axis=2, tiled=True),
        lax.all_gather(w_out, "node", axis=2, tiled=True),
    )
    w_query = qkv_whole[0, 0]
    w_key = qkv_whole[0, 1]
    w_value = qkv_whole[0, 2]
    w_proj = out_whole[0]
    gain_row = gain[0]
    rows = feats.shape[1]
    carried = jnp.zeros_like(feats[0])
    results = []
    for tick in range(MICRO + 1):
        micro = jnp.clip(tick - segment, 0, MICRO - 1)
        fresh = feats[min(tick, MICRO - 1)]
        inputs = jnp.where(segment == 0, fresh, carried)
        whole = lax.all_gather(inputs, "head", axis=1, tiled=True)
        xf = whole.astype(jnp.float32)
        inv = lax.rsqrt(jnp.mean(xf * xf, axis=-1, keepdims=True) + EPS)
        normed = (xf * inv * gain_row).astype(jnp.bfloat16)
        query = jnp.dot(normed, w_query, preferred_element_type=jnp.float32).astype(jnp.bfloat16)
        key = jnp.dot(normed, w_key, preferred_element_type=jnp.float32).astype(jnp.bfloat16)
        value = jnp.dot(normed, w_value, preferred_element_type=jnp.float32).astype(jnp.bfloat16)
        mask_rows = lax.dynamic_index_in_dim(block_mask, micro, 0, keepdims=False)
        own_flag = mask_rows[me, me] > 0
        key_list = [key]
        value_list = [value]
        flag_list = [own_flag]
        for bit in bit_list:
            far_key, far_value = from_partner((key, value), "node", bit)
            key_list.append(far_key)
            value_list.append(far_value)
            flag_list.append(mask_rows[me, jnp.bitwise_xor(me, 1 << bit)] > 0)
        keep = jnp.repeat(jnp.stack(flag_list), rows)
        summed, top, total = partial_attend(
            query, jnp.concatenate(key_list, 0), jnp.concatenate(value_list, 0), keep
        )
        attended = finish(summed, total)
        terms = jnp.dot(attended, w_proj, preferred_element_type=jnp.float32)
        reduced = lax.psum_scatter(
            terms.astype(jnp.bfloat16), "head", scatter_dimension=1, tiled=True
        ).astype(jnp.float32)
        output = (inputs.astype(jnp.float32) + reduced).astype(jnp.bfloat16)
        results.append(output)
        if tick < MICRO:
            carried = from_behind(output, "pipe", 1)
    first = jnp.where(segment == 0, results[0], results[1])
    second = jnp.where(segment == 0, results[1], results[2])
    return jnp.stack([first, second])[None]


PIECES = 4
MESH_ID = pl.DeviceIdType.MESH
ANY = pl.BlockSpec(memory_space=pl.ANY)


def place():
    core, node, y = lax.axis_index("pipe"), lax.axis_index("node"), lax.axis_index("head")
    return core, lax.rem(node, 2), y, lax.div(node, 2)


def dev(core, x, y, z):
    return (core, z * 2 + x, y)


def z_apart(z, d):
    if d == 0:
        return z
    if d == 1:
        return z + 1 - 2 * lax.rem(z, 2)
    if d == 2:
        return z + 2 - 4 * lax.div(z, 2)
    return 3 - z


def remote(src, dst, send, recv, target):
    return pltpu.make_async_remote_copy(
        src_ref=src, dst_ref=dst, send_sem=send, recv_sem=recv, device_id=target, device_id_type=MESH_ID
    )


def greet(peers):
    barrier = pltpu.get_barrier_semaphore()
    for peer in peers:
        pl.semaphore_signal(barrier, inc=1, device_id=peer, device_id_type=MESH_ID)
    pl.semaphore_wait(barrier, len(peers))


def head_slot(core, y, z):
    return 8 * y + 2 * z + core


def column_slot(core, y, z):
    return 4 * z + 2 * y + core


class Gather:
    def __init__(self, slot, own, out, sems, sent):
        self.slot, self.own, self.out, self.sent = slot, own, out, sent
        self.local, self.zs, self.zr, self.ys, self.yr, self.bs, self.br = sems
        self.at = place()
        self.rows, self.wide = own.shape[0] // PIECES, own.shape[1]
        core, x, y, z = self.at
        self.far = [dev(core, x, y, z_apart(z, d)) for d in (1, 2, 3)]
        self.beside, self.sibling = dev(core, x, 1 - y, z), dev(1 - core, x, y, z)

    def peers(self):
        return self.far + [self.beside, self.sibling]

    def mine(self, p):
        return self.own.at[pl.ds(p * self.rows, self.rows), :]

    def region(self, c, yy, zz, p):
        column = pl.multiple_of(self.slot(c, yy, zz) * self.wide, self.wide)
        return self.out.at[pl.ds(p * self.rows, self.rows), pl.ds(column, self.wide)]

    def send(self, src, dst, ssem, rsem, target):
        copy = remote(src, dst, ssem, rsem, target)
        copy.start()
        self.sent.append(copy.wait_send)

    def await_recv(self, got, sem):
        remote(self.mine(0), got, sem, sem, self.sibling).wait_recv()

    def start(self, p):
        core, x, y, z = self.at
        mine, spot = self.mine(p), self.region(core, y, z, p)
        for d in (1, 2, 3):
            self.send(mine, spot, self.zs.at[p, d - 1], self.zr.at[p, d - 1], self.far[d - 1])
        self.send(mine, spot, self.ys.at[p, 0], self.yr.at[p, 0], self.beside)
        self.send(mine, spot, self.bs.at[p, 0], self.br.at[p, 0], self.sibling)
        pltpu.make_async_copy(mine, spot, self.local.at[p]).start()

    def along_z(self, p):
        core, x, y, z = self.at
        for d in (1, 2, 3):
            got = self.region(core, y, z_apart(z, d), p)
            self.await_recv(got, self.zr.at[p, d - 1])
            self.send(got, got, self.ys.at[p, d], self.yr.at[p, d], self.beside)
            self.send(got, got, self.bs.at[p, d], self.br.at[p, d], self.sibling)

    def along_y(self, p):
        core, x, y, z = self.at
        for d in range(4):
            got = self.region(core, 1 - y, z_apart(z, d), p)
            self.await_recv(got, self.yr.at[p, d])
            self.send(got, got, self.bs.at[p, 4 + d], self.br.at[p, 4 + d], self.sibling)

    def whole(self, p):
        core, x, y, z = self.at
        for d in range(8):
            got = self.region(1 - core, y if d < 4 else 1 - y, z_apart(z, d % 4), p)
            self.await_recv(got, self.br.at[p, d])
        pltpu.make_async_copy(self.mine(p), self.region(core, y, z, p), self.local.at[p]).wait()


def gather_sems():
    dma = pltpu.SemaphoreType.DMA
    return [dma((PIECES,))] + [dma((PIECES, c)) for c in (3, 3, 4, 4, 8, 8)]


def own_columns(array):
    core, x, y, z = place()
    return array.at[:, pl.ds(pl.multiple_of(column_slot(core, y, z) * HD, HD), HD)]


def project_piece(all_ref, wo_ref, s, rest_ref, into_ref, p):
    rows = all_ref.shape[0] // PIECES
    span = slice(p * rows, (p + 1) * rows)
    projected = jnp.dot(all_ref[span, :], wo_ref[s], preferred_element_type=jnp.float32)
    into_ref[span, :] = (rest_ref[span, :].astype(jnp.float32) + projected).astype(jnp.bfloat16)


def main_kernel(
    feats, gain, w_qkv, w_out, flags, mid, out_ref, wo,
    xg, gains, wq, all_ref, own, rest_ref, into_ref, q_ref, k_ref, v_ref,
    l_sem, x_send, x_recv, z_send, z_recv, y_send, y_recv, b_send, b_recv,
    g_send, g_recv, q_send, q_recv, qx_send, qx_recv, o_send, o_recv, rest_sem, *sems,
):
    core, x, y, z = place()
    node = z * 2 + x
    half, wide = feats.shape[1] // 2, feats.shape[2]
    depth = w_qkv.shape[2]
    far = [z_apart(z, d) for d in (1, 2, 3)]
    beside, sibling, across = dev(core, x, 1 - y, z), dev(1 - core, x, y, z), dev(core, 1 - x, y, z)
    plane = [
        dev(cc, xx, yy, z)
        for cc in (core, 1 - core)
        for xx in (x, 1 - x)
        for yy in (y, 1 - y)
    ][1:]
    greet(plane + [dev(cc, x, y, zz) for zz in far for cc in (core, 1 - core)])
    sent = []
    local = []

    def send(src, dst, ssem, rsem, target):
        copy = remote(src, dst, ssem, rsem, target)
        copy.start()
        sent.append(copy)

    def keep(src, dst, sem):
        copy = pltpu.make_async_copy(src, dst, sem)
        copy.start()
        local.append(copy)

    def region(c, xx, yy, zz):
        return xg.at[
            pl.ds(pl.multiple_of((zz * 2 + xx) * 2 * half + c * half, half), half),
            pl.ds(pl.multiple_of(yy * wide, wide), wide),
        ]

    rows = pl.ds(pl.multiple_of(core * half, half), half)
    mine, other = feats.at[x, rows, :], feats.at[1 - x, rows, :]
    spot = region(core, x, y, z)
    send(other, spot, x_send, x_recv, across)
    send(mine, spot, y_send.at[0], y_recv.at[0], beside)
    for d in (1, 2, 3):
        send(mine, spot, z_send.at[d - 1], z_recv.at[d - 1], dev(core, x, y, far[d - 1]))
    send(mine, spot, b_send.at[0], b_recv.at[0], sibling)
    keep(mine, spot, l_sem.at[0])
    send(gain, gains.at[core], g_send, g_recv, sibling)
    keep(gain, gains.at[core], l_sem.at[1])

    far_x = region(core, 1 - x, y, z)
    remote(mine, far_x, x_send, x_recv, sibling).wait_recv()
    send(far_x, far_x, y_send.at[4], y_recv.at[4], beside)
    for d in (1, 2, 3):
        send(far_x, far_x, z_send.at[2 + d], z_recv.at[2 + d], dev(core, x, y, far[d - 1]))
    send(far_x, far_x, b_send.at[8], b_recv.at[8], sibling)

    def head_columns(zz, c):
        return w_qkv.at[0, :, :, pl.ds(pl.multiple_of((zz * 2 + c) * HD, HD), HD)]

    def depth_rows(c, xx, zz):
        return wq.at[c, :, pl.ds(pl.multiple_of((zz * 2 + xx) * depth, depth), depth), :]

    own_rows = depth_rows(core, x, z)
    weights = []
    for d in range(4):
        zz = z_apart(z, d)
        for other_core in range(2):
            target = 1 - core if other_core else core
            if d == 0 and not other_core:
                keep(head_columns(z, core), own_rows, l_sem.at[2])
                weights.append(remote(head_columns(z, core), own_rows, qx_send.at[0], qx_recv.at[0], across))
            else:
                at = 2 * d + other_core
                weights.append(
                    remote(head_columns(zz, target), own_rows, q_send.at[at], q_recv.at[at], dev(target, x, y, zz))
                )

    def start_weights():
        for copy in weights:
            copy.start()

    def pass_section(s):
        for d in range(4):
            at = 2 * d + (core if s == 0 else 1 - core)
            got = depth_rows(s, x, z_apart(z, d))
            arrived = remote(head_columns(z, core), got, x_send, q_recv.at[at], sibling)
            if d:
                arrived.wait_recv()
                send(got, got, qx_send.at[at], qx_recv.at[at], across)
            else:
                copy = remote(got, got, qx_send.at[1], qx_recv.at[1], across)

                @pl.when(core != s)
                def _():
                    arrived.wait_recv()
                    copy.start()

                if s == 0:
                    weights.append(copy)

    def await_section(s):
        for d in range(4):
            at = 2 * d + (core if s == 0 else 1 - core)
            got = depth_rows(s, 1 - x, z_apart(z, d))
            remote(head_columns(z, core), got, x_send, qx_recv.at[at], sibling).wait_recv()

    def await_projection():
        for yy in range(2):
            for cc in range(2):
                got = wo.at[cc, pl.ds(yy * half_rows, half_rows), :]
                remote(w_out.at[0, :, pl.ds(0, HD)], got, x_send, o_recv.at[2 * yy + cc], sibling).wait_recv()

    pl.when(core == 0)(start_weights)
    for k in range(2):
        xx = 1 - x if k else x
        for d in (1, 2, 3):
            got = region(core, xx, y, far[d - 1])
            remote(mine, got, x_send, z_recv.at[3 * k + d - 1], sibling).wait_recv()
            send(got, got, y_send.at[4 * k + d], y_recv.at[4 * k + d], beside)
            send(got, got, b_send.at[8 * k + d], b_recv.at[8 * k + d], sibling)
    pl.when(core == 1)(start_weights)
    pass_section(0)
    for k in range(2):
        xx = 1 - x if k else x
        for d in range(4):
            got = region(core, xx, 1 - y, z_apart(z, d))
            remote(mine, got, x_send, y_recv.at[4 * k + d], sibling).wait_recv()
            send(got, got, b_send.at[8 * k + 4 + d], b_recv.at[8 * k + 4 + d], sibling)
    for k in range(2):
        xx = 1 - x if k else x
        for d in range(8):
            got = region(1 - core, xx, y if d < 4 else 1 - y, z_apart(z, d % 4))
            remote(mine, got, x_send, b_recv.at[8 * k + d], sibling).wait_recv()
    half_rows = w_out.shape[1]
    to = wo.at[core, pl.ds(pl.multiple_of(y * half_rows, half_rows), half_rows), :]
    projections = []
    for a in range(2):
        for b in range(2):
            xx = 1 - x if a else x
            cc = 1 - core if b else core
            src = w_out.at[0, :, pl.ds(pl.multiple_of(cc * HD, HD), HD)]
            rsem = o_recv.at[2 * y + core]
            copy = remote(src, to, o_send.at[2 * a + b], rsem, dev(cc, xx, x, z))
            if a == 0 and b == 0:
                pl.when(x != y)(copy.start)
                pl.when(x == y)(pltpu.make_async_copy(src, to, rsem).start)
            else:
                copy.start()
            projections.append(copy)

    remote(gain, gains.at[1 - core], g_send, g_recv, sibling).wait_recv()
    for copy in local:
        copy.wait()
    await_section(0)
    rest = pltpu.make_async_copy(own_columns(xg), rest_ref, rest_sem)
    rest.start()
    for p in range(PIECES):
        span = pl.ds(p * (xg.shape[0] // PIECES), xg.shape[0] // PIECES)
        project_rows(
            xg[span, :].astype(jnp.float32), gains[0], lambda part: wq[0, part], (q_ref, k_ref, v_ref), span
        )
    attend_blocks(q_ref, k_ref, v_ref, flags, own)
    rest.wait()
    waits = []
    heads = Gather(head_slot, own, all_ref, sems[:7], waits)
    columns = Gather(column_slot, into_ref, mid, sems[7:], waits)
    for p in range(PIECES):
        heads.start(p)
    pass_section(1)
    rows = mid.shape[0] // PIECES
    for step in range(2 * PIECES + 2):
        for stage in range(3):
            part = step - stage
            if part < 0 or part >= 2 * PIECES:
                continue
            gather, p = (heads, part) if part < PIECES else (columns, part - PIECES)
            if stage == 0:
                gather.along_z(p)
            elif stage == 1:
                gather.along_y(p)
            else:
                gather.whole(p)
                if part == 0:
                    await_projection()
                if part == PIECES:
                    await_section(1)
                if gather is heads:
                    project_piece(all_ref, wo, 0, rest_ref, into_ref, p)
                    columns.start(p)
                else:
                    span = pl.ds(p * rows, rows)
                    project_rows(
                        mid[span, :].astype(jnp.float32), gains[1], lambda part: wq[1, part],
                        (q_ref, k_ref, v_ref), span,
                    )
    attend_blocks(q_ref, k_ref, v_ref, flags, out_ref)
    for copy in sent + weights:
        copy.wait_send()
    pl.when(x != y)(projections[0].wait_send)
    for copy in projections[1:]:
        copy.wait_send()
    for wait in waits:
        wait()


def first_layer(feats, gain, w_qkv, w_out, flags):
    dma = pltpu.SemaphoreType.DMA
    vmem = pl.BlockSpec(memory_space=pltpu.VMEM)
    bf = jnp.bfloat16
    rows, wide = feats.shape[1] * 8, feats.shape[2] * 2
    narrow = pltpu.VMEM((rows, HD), bf)
    return pl.pallas_call(
        main_kernel,
        out_shape=(
            jax.ShapeDtypeStruct((rows, wide), bf),
            jax.ShapeDtypeStruct((rows, HD), bf),
            jax.ShapeDtypeStruct((2, wide, HD), bf),
        ),
        in_specs=[ANY] * 4 + [pl.BlockSpec(memory_space=pltpu.SMEM)],
        out_specs=(vmem,) * 3,
        scratch_shapes=[pltpu.VMEM((rows, wide), bf), pltpu.VMEM((2, 1, wide), jnp.float32),
                        pltpu.VMEM((2, 3, wide, HD), bf), pltpu.VMEM((rows, wide), bf)] + [narrow] * 6
        + [dma((3,)), dma(()), dma(()), dma((6,)), dma((6,)), dma((8,)), dma((8,)), dma((16,)), dma((16,)),
           dma(()), dma(()), dma((8,)), dma((8,)), dma((8,)), dma((8,)), dma((4,)), dma((4,)), dma(())]
        + gather_sems() + gather_sems(),
        compiler_params=pltpu.CompilerParams(
            collective_id=0, has_side_effects=True, vmem_limit_bytes=63 * 2**20
        ),
        name="first_layer",
    )(feats, gain, w_qkv, w_out, flags)


def finish_kernel(
    own, mid, wo_ref, out,
    all_ref, rest_ref, last, rest_sem, l_sem, m_send, m_recv, a_send, a_recv, *sems,
):
    sent = []
    heads = Gather(head_slot, own, all_ref, sems, sent)
    core, x, y, z = place()
    node = z * 2 + x
    rows, wide = out.shape[1], out.shape[2]
    piece = last.shape[1]
    to_y = lax.div(z, 2)
    z_low = lax.rem(z, 2)
    first = core == 0
    to_self = (core == 1) & (y == to_y)
    barrier = pltpu.get_barrier_semaphore()

    def signal(peer):
        pl.semaphore_signal(barrier, inc=1, device_id=peer, device_id_type=MESH_ID)

    for peer in heads.peers():
        signal(peer)

    @pl.when(first)
    def _():
        signal(dev(0, 1 - x, y, z))

    sources = [(zl, xx, yy, cc) for zl in range(2) for xx in range(2) for yy in range(2) for cc in range(2)]
    for zl, xx, yy, cc in sources:
        own = (cc == core) & (xx == x) & (yy == y) & (2 * y + zl == z)

        @pl.when((core == 1) & jnp.logical_not(own))
        def _():
            signal(dev(cc, xx, yy, 2 * y + zl))

    pl.semaphore_wait(barrier, 13 - to_self.astype(jnp.int32) + first.astype(jnp.int32))

    for p in range(PIECES):
        heads.start(p)
    rest = pltpu.make_async_copy(own_columns(mid), rest_ref, rest_sem)
    rest.start()

    def mid_rows(n):
        return mid.at[
            pl.ds(pl.multiple_of(n * rows, rows), rows), pl.ds(pl.multiple_of(y * wide, wide), wide)
        ]

    cross = remote(mid_rows(z * 2 + 1 - x), out.at[x], m_send, m_recv, dev(0, 1 - x, y, z))
    keep = pltpu.make_async_copy(mid_rows(node), out.at[x], l_sem)

    @pl.when(first)
    def _():
        cross.start()
        keep.start()

    slot = 4 * z_low + 2 * y + core
    spot = out.at[x, :, pl.ds(pl.multiple_of(slot * piece, piece), piece)]
    index = 8 * z_low + 4 * x + 2 * y + core
    copies = []
    rest.wait()
    for step in range(PIECES + 2):
        if step < PIECES:
            heads.along_z(step)
        if 0 <= step - 1 < PIECES:
            heads.along_y(step - 1)
        p = step - 2
        if p < 0:
            continue
        heads.whole(p)
        project_piece(all_ref, wo_ref, 1, rest_ref, last, p)
        for n in range(8 // PIECES * p, 8 // PIECES * (p + 1)):
            src = last.at[pl.ds(n * rows, rows), :]
            copy = remote(src, spot, a_send.at[n], a_recv.at[index], dev(1, n % 2, to_y, n // 2))
            mine = to_self & (node == n)
            pl.when(jnp.logical_not(mine))(copy.start)
            pl.when(mine)(pltpu.make_async_copy(src, spot, a_recv.at[index]).start)
            copies.append((copy, mine))

    @pl.when(first)
    def _():
        remote(mid_rows(node), out.at[1 - x], m_send, m_recv, dev(0, 1 - x, y, z)).wait_recv()
        cross.wait_send()
        keep.wait()

    @pl.when(core == 1)
    def _():
        for zl, xx, yy, cc in sources:
            at = 4 * zl + 2 * yy + cc
            got = out.at[xx, :, pl.ds(at * piece, piece)]
            remote(
                last.at[pl.ds(0, rows), :], got, a_send.at[0], a_recv.at[8 * zl + 4 * xx + 2 * yy + cc],
                dev(0, x, y, z),
            ).wait_recv()

    for copy, mine in copies:
        pl.when(jnp.logical_not(mine))(copy.wait_send)
    for wait in sent:
        wait()


def finish_layers(own, mid, wo):
    dma = pltpu.SemaphoreType.DMA
    rows, wide = mid.shape
    narrow = pltpu.VMEM((rows, HD), jnp.bfloat16)
    return pl.pallas_call(
        finish_kernel,
        out_shape=jax.ShapeDtypeStruct((2, rows // 8, wide // 2), mid.dtype),
        in_specs=[ANY, ANY, pl.BlockSpec(memory_space=pltpu.VMEM)],
        out_specs=ANY,
        scratch_shapes=[pltpu.VMEM((rows, wide), jnp.bfloat16), narrow, narrow]
        + [dma(()), dma(()), dma(()), dma(()), dma((8,)), dma((16,))] + gather_sems(),
        compiler_params=pltpu.CompilerParams(
            collective_id=3, has_side_effects=True, vmem_limit_bytes=63 * 2**20
        ),
        name="finish",
    )(own, mid, wo)


def project_rows(xf, gain_row, w_part, refs, here):
    inv = lax.rsqrt(jnp.mean(xf * xf, axis=-1, keepdims=True) + EPS)
    normed = (xf * inv * gain_row).astype(jnp.bfloat16)
    for part, ref in enumerate(refs):
        ref[here, :] = jnp.dot(normed, w_part(part), preferred_element_type=jnp.float32).astype(jnp.bfloat16)


def attend_blocks(q_ref, k_ref, v_ref, flags, out_ref):
    count = flags.shape[0]
    rows = q_ref.shape[0] // count
    width = count.bit_length() - 1
    bits = [width - 1, width // 2, 0]
    for block in range(count):
        seen = [block] + [block ^ (1 << bit) for bit in bits]
        span = slice(block * rows, (block + 1) * rows)
        query = q_ref[span, :]
        scores = []
        for other in seen:
            key = k_ref[other * rows : (other + 1) * rows, :]
            dots = lax.dot_general(query, key, (((1,), (1,)), ((), ())), preferred_element_type=jnp.float32)
            scores.append(jnp.where(flags[block, other] > 0, dots * (1.0 / HD**0.5), NEG))
        top = functools.reduce(jnp.maximum, [jnp.max(s, axis=-1, keepdims=True) for s in scores])
        total = jnp.zeros_like(top)
        summed = jnp.zeros((rows, HD), jnp.float32)
        for other, s in zip(seen, scores):
            expo = jnp.where(flags[block, other] > 0, jnp.exp(s - top), 0.0)
            total = total + jnp.sum(expo, axis=-1, keepdims=True)
            summed = summed + jnp.dot(
                expo.astype(jnp.bfloat16), v_ref[other * rows : (other + 1) * rows, :],
                preferred_element_type=jnp.float32,
            )
        out_ref[span, :] = (summed / total).astype(jnp.bfloat16)


def local_planes(feats, gain, w_qkv, w_out, block_mask):
    core, micro, y, z = place()
    flags = lax.dynamic_index_in_dim(block_mask, micro, 0, keepdims=False)
    mid, attended, wo = first_layer(feats, gain, w_qkv, w_out, flags)
    return finish_layers(attended, mid, wo)[None]


def solution(mesh):
    planes = (mesh.shape["pipe"], mesh.shape["node"], mesh.shape["head"]) == (2, 8, 2)
    return jax.shard_map(
        local_planes if planes else local_any,
        mesh=mesh,
        in_specs=(
            P(None, "node", "head"),
            P("pipe", None),
            P("pipe", None, "node", "head"),
            P("pipe", "head", "node"),
            P(),
        ),
        out_specs=P("pipe", None, "node", "head"),
        check_vma=False,
    )
```

profile of v0, /device:TPU:25, one launch (start us, length us, event | category | flops | bytes accessed | tf_op | source)
XLA Modules:
  0.0 180.2 jit_solution(3305561126659660808)
XLA Ops:
  0.0 0.0 copy-start
  0.0 0.7 copy-done
  0.7 0.6 dynamic-slice_bitcast_fusion.flags
  1.3 131.2 %first_layer.1 = (bf16[1024,2048]{1,0:T(8,128)(2,1)}, bf16[1024,128]{1,0:T(8,128)(2,1)}, bf16[2,2048,128]{2,1,0:T(8,128)(2,1)}) custom-call(bf16[2,128,1024]{2,1,0:T(8,128)(2,1)} %feats.1, f32[1,2048]{1,0:T(1,128)} %gain.1, bf16[1,3,256,1024]{3,2,1,0:T(8,128)(2,1)} %w_qkv.1, bf16[1,1024,256]{2,1,0:T(8,128)(2,1)} %w_out.1, s32[8,8]{1,0:T(8,128)} %dynamic-slice_bitcast_fusion.flags), custom_call_target="tpu_custom_call" | custom-call | tf_op jit(solution)/shard_map/first_layer/pallas_call | solution.py:448
  132.5 45.8 %finish.1 = bf16[2,128,1024]{2,1,0:T(8,128)(2,1)} custom-call(bf16[1024,128]{1,0:T(8,128)(2,1)} %get-tuple-element.8.own, bf16[1024,2048]{1,0:T(8,128)(2,1)} %get-tuple-element.9.mid, bf16[2,2048,128]{2,1,0:T(8,128)(2,1)} %get-tuple-element.10.wo_ref), custom_call_target="tpu_custom_call" | custom-call | tf_op jit(solution)/shard_map/finish/pallas_call | solution.py:572
  178.3 1.9 %copy.7 = bf16[1,2,128,1024]{3,2,1,0:T(8,128)(2,1)} copy(bf16[1,2,128,1024]{3,2,1,0:T(8,128)(2,1)} %bitcast.3) | data formatting | bytes 1048576
Async XLA Ops:
  0.0 0.7 copy-start
where the time goes:
time: 180 us
  Pallas kernels  177 us (98%)
  local copies, waits for them, and re-layouts  3.16 us (2%)
    pallas_call x1, Pallas kernels, first_layer(): pl.pallas_call(main_kernel, out_shape=(jax.ShapeDtypeStruct((rows, wide),...  131 us
    pallas_call x1, Pallas kernels, finish_layers(): pl.pallas_call(finish_kernel, out_shape=jax.ShapeDtypeStruct((2, rows //...  45.8 us

commit v1 on v0

v1 whole, which is shorter than its diff:
```python
import functools
import jax
import jax.numpy as jnp
from jax import lax
from jax.experimental import pallas as pl
from jax.experimental.pallas import tpu as pltpu
from jax.sharding import PartitionSpec as P

HD = 128
MICRO = 2


EPS = 1e-06
NEG = -1e30


def from_partner(block, axis, apart):
    count = lax.axis_size(axis)
    route = []
    for low in range(count):
        high = low | 1 << apart
        if high != low and high < count:
            route += [(low, high), (high, low)]
    return lax.ppermute(block, axis, route)


def from_behind(value, axis, steps):
    count = lax.axis_size(axis)
    first, last = (max(0, -steps), min(count, count - steps))
    return lax.ppermute(value, axis, [(source, source + steps) for source in range(first, last)])


def partial_attend(query, key, value, keep):
    rows = query.shape[0]
    groups = query.shape[1] // HD
    q_heads = query.reshape(rows, groups, HD)
    k_heads = key.reshape(key.shape[0], groups, HD)
    v_heads = value.reshape(value.shape[0], groups, HD)
    scores = jnp.einsum("qhd,khd->hqk", q_heads, k_heads, preferred_element_type=jnp.float32) * (
        1.0 / HD**0.5
    )
    scores = jnp.where(keep[None, None, :], scores, NEG)
    top = jnp.max(scores, axis=-1)
    expo = jnp.where(keep[None, None, :], jnp.exp(scores - top[..., None]), 0.0)
    total = jnp.sum(expo, axis=-1)
    summed = jnp.einsum(
        "hqk,khd->hqd", expo.astype(jnp.bfloat16), v_heads, preferred_element_type=jnp.float32
    )
    return (summed, top, total)


def finish(summed, total):
    out = summed / total[..., None]
    rows = out.shape[1]
    return jnp.transpose(out, (1, 0, 2)).reshape(rows, -1).astype(jnp.bfloat16)


def local_any(feats, gain, w_qkv, w_out, block_mask):
    segment = lax.axis_index("pipe")
    me = lax.axis_index("node")
    width = lax.axis_size("node").bit_length() - 1
    bit_list = [width - 1, width // 2, 0]
    qkv_whole, out_whole = (
        lax.all_gather(w_qkv, "node", axis=2, tiled=True),
        lax.all_gather(w_out, "node", axis=2, tiled=True),
    )
    w_query = qkv_whole[0, 0]
    w_key = qkv_whole[0, 1]
    w_value = qkv_whole[0, 2]
    w_proj = out_whole[0]
    gain_row = gain[0]
    rows = feats.shape[1]
    carried = jnp.zeros_like(feats[0])
    results = []
    for tick in range(MICRO + 1):
        micro = jnp.clip(tick - segment, 0, MICRO - 1)
        fresh = feats[min(tick, MICRO - 1)]
        inputs = jnp.where(segment == 0, fresh, carried)
        whole = lax.all_gather(inputs, "head", axis=1, tiled=True)
        xf = whole.astype(jnp.float32)
        inv = lax.rsqrt(jnp.mean(xf * xf, axis=-1, keepdims=True) + EPS)
        normed = (xf * inv * gain_row).astype(jnp.bfloat16)
        query = jnp.dot(normed, w_query, preferred_element_type=jnp.float32).astype(jnp.bfloat16)
        key = jnp.dot(normed, w_key, preferred_element_type=jnp.float32).astype(jnp.bfloat16)
        value = jnp.dot(normed, w_value, preferred_element_type=jnp.float32).astype(jnp.bfloat16)
        mask_rows = lax.dynamic_index_in_dim(block_mask, micro, 0, keepdims=False)
        own_flag = mask_rows[me, me] > 0
        key_list = [key]
        value_list = [value]
        flag_list = [own_flag]
        for bit in bit_list:
            far_key, far_value = from_partner((key, value), "node", bit)
            key_list.append(far_key)
            value_list.append(far_value)
            flag_list.append(mask_rows[me, jnp.bitwise_xor(me, 1 << bit)] > 0)
        keep = jnp.repeat(jnp.stack(flag_list), rows)
        summed, top, total = partial_attend(
            query, jnp.concatenate(key_list, 0), jnp.concatenate(value_list, 0), keep
        )
        attended = finish(summed, total)
        terms = jnp.dot(attended, w_proj, preferred_element_type=jnp.float32)
        reduced = lax.psum_scatter(
            terms.astype(jnp.bfloat16), "head", scatter_dimension=1, tiled=True
        ).astype(jnp.float32)
        output = (inputs.astype(jnp.float32) + reduced).astype(jnp.bfloat16)
        results.append(output)
        if tick < MICRO:
            carried = from_behind(output, "pipe", 1)
    first = jnp.where(segment == 0, results[0], results[1])
    second = jnp.where(segment == 0, results[1], results[2])
    return jnp.stack([first, second])[None]


MESH_ID = pl.DeviceIdType.MESH
ANY = pl.BlockSpec(memory_space=pl.ANY)
PAIR = 2 * HD
KEY, QUERY, VALUE = 1, 0, 2


def place():
    core, node, y = lax.axis_index("pipe"), lax.axis_index("node"), lax.axis_index("head")
    return core, lax.rem(node, 2), y, lax.div(node, 2)


def dev(core, x, y, z):
    return (core, z * 2 + x, y)


def z_apart(z, d):
    if d == 0:
        return z
    if d == 1:
        return z + 1 - 2 * lax.rem(z, 2)
    if d == 2:
        return z + 2 - 4 * lax.div(z, 2)
    return 3 - z


def remote(src, dst, send, recv, target):
    return pltpu.make_async_remote_copy(
        src_ref=src, dst_ref=dst, send_sem=send, recv_sem=recv, device_id=target, device_id_type=MESH_ID
    )


def greet(peers):
    barrier = pltpu.get_barrier_semaphore()
    for peer in peers:
        pl.semaphore_signal(barrier, inc=1, device_id=peer, device_id_type=MESH_ID)
    pl.semaphore_wait(barrier, len(peers))


def relay_kernel(
    feats, gain, w_qkv, w_out, mask, out,
    xg, normed, gains, wq, wo, q_ref, k_ref, v_ref, e_ref, t_ref, attg, own_part, send_part, recv_part,
    rest, midg, fin, snd, rcv, w_sem, o_sem, f_sem, loc,
):
    core, x, y, z = place()
    zh, zl = lax.div(z, 2), lax.rem(z, 2)
    half = core + zh - 2 * core * zh
    rows, wide = feats.shape[1], feats.shape[2]
    depth = w_qkv.shape[2]
    tile = 2 * zl + x
    pair = 4 * y + tile
    sibling, over = dev(1 - core, x, y, z), z_apart(z, 2)
    partner = {"x": dev(core, 1 - x, y, z), "y": dev(core, x, 1 - y, z), "z": dev(core, x, y, z_apart(z, 1))}
    greet(
        [
            dev(cc, xx, y, z_apart(z, d))
            for d in range(4)
            for xx in (x, 1 - x)
            for cc in (core, 1 - core)
        ][1:]
        + [partner["y"]]
    )
    names, sent, local = {}, [], []

    def arrival(key):
        return rcv.at[names.setdefault(key, len(names))]

    def make(src, dst, sem, target):
        copy = remote(src, dst, snd.at[len(sent)], sem, target)
        sent.append((copy, None))
        return copy

    def push(src, dst, sem, target, when=None):
        copy = remote(src, dst, snd.at[len(sent)], sem, target)
        sent.append((copy, when))
        if when is None:
            copy.start()
        else:
            pl.when(when)(copy.start)

    def arrive(dst, sem):
        remote(dst, dst, snd.at[0], sem, sibling).wait_recv()

    def keep(src, dst, sem):
        copy = pltpu.make_async_copy(src, dst, sem)
        copy.start()
        local.append(copy)

    class Spread:
        def __init__(self, tag, order, region):
            self.tag, self.order, self.region = tag, order, region

        def at(self, off):
            return self.region(
                1 - x if "x" in off else x, 1 - y if "y" in off else y, 1 - zl if "z" in off else zl
            )

        def key(self, off):
            return arrival((self.tag, "".join(sorted(off))))

        def pass_on(self, off, dims):
            spot = self.at(off)
            for d in dims:
                push(spot, spot, self.key(off + d), partner[d])

        def start(self):
            self.pass_on("", self.order)

        def take(self, off):
            arrive(self.at(off), self.key(off))
            last = max(self.order.index(d) for d in off)
            self.pass_on(off, self.order[last + 1 :])

        def stage(self, i):
            d = self.order[i]
            for n in range(1 << i):
                self.take("".join(self.order[b] for b in range(i) if n >> b & 1) + d)

    def weight_copies(part):
        copies = []
        to = wq.at[core, part, pl.ds(pl.multiple_of((2 * z + x) * depth, depth), depth), :]
        for d in (2, 3, 1, 0):
            for xx in (1 - x, x):
                zz = z_apart(z, d)
                spot = pl.multiple_of((2 * lax.rem(zz, 2) + xx) * PAIR, PAIR)
                src = w_qkv.at[0, part, :, pl.ds(spot, PAIR)]
                if d == 0 and xx is x:
                    copies.append(pltpu.make_async_copy(src, to, w_sem.at[core, part]))
                else:
                    copies.append(make(src, to, w_sem.at[core, part], dev(core, xx, y, zz)))
        return copies

    weights = {part: weight_copies(part) for part in (KEY, QUERY, VALUE)}
    own_wo = wo.at[core, zh]
    wo_copies = [
        make(w_out.at[0], own_wo, o_sem.at[core, zh], dev(core, x, y, over)),
        make(w_out.at[0], own_wo, o_sem.at[core, zh], sibling),
        pltpu.make_async_copy(w_out.at[0], own_wo, o_sem.at[core, zh]),
    ]

    def begin(copies, section):
        @pl.when(core == section)
        def _():
            for copy in copies:
                copy.start()

    def await_weights(s, part):
        got = wq.at[s, part]
        arrive(got, w_sem.at[s, part])
        push(got, got, w_sem.at[s, part], sibling, core == s)

    def await_projection(s):
        arrive(wo.at[s, zh], o_sem.at[s, zh])
        got = wo.at[s, 1 - zh]
        arrive(got, o_sem.at[s, 1 - zh])
        push(got, got, o_sem.at[s, 1 - zh], sibling, core == s)

    own_spot = xg.at[y, pl.ds(pl.multiple_of(tile * rows, rows), rows), :]
    own_key = arrival("own")
    cross = make(feats.at[1 - zh], own_spot, own_key, dev(core, x, y, over))
    sent.pop()
    sent.append((cross, core == 1))
    pl.when(core == 1)(cross.start)
    pl.when(core == 0)(pltpu.make_async_copy(feats.at[zh], own_spot, own_key).start)
    push(gain, gains.at[core], arrival("gain"), sibling)
    keep(gain, gains.at[core], loc.at[0])
    arrive(own_spot, own_key)
    cut = rows // 2
    fs = [
        Spread(
            ("f", p), "zxy",
            lambda xx, yy, zz, p=p: xg.at[yy, pl.ds(pl.multiple_of((2 * zz + xx) * rows + p * cut, cut), cut), :],
        )
        for p in range(2)
    ]
    for f in fs:
        f.start()
    begin(weights[KEY], 0)
    for f in fs:
        f.stage(0)
    begin(weights[QUERY], 0)
    for f in fs:
        f.stage(1)
    begin(weights[VALUE] + wo_copies, 0)
    for f in fs:
        f.stage(2)
    arrive(gains.at[1 - core], arrival("gain"))
    local[0].wait()
    rest_copy = pltpu.make_async_copy(
        xg.at[y, :, pl.ds(pl.multiple_of(tile * PAIR, PAIR), PAIR)], rest, loc.at[1]
    )
    rest_copy.start()

    chunk = 16

    def normalize(load, width, count, s, first, length):
        def body(i, carry):
            span = pl.ds(pl.multiple_of(first + i * chunk, chunk), chunk)
            xs = [load(n, span).astype(jnp.float32) for n in range(count)]
            squares = functools.reduce(jnp.add, [jnp.sum(v * v, axis=-1, keepdims=True) for v in xs])
            inv = lax.rsqrt(squares * (1.0 / (width * count)) + EPS)
            for n, v in enumerate(xs):
                cols = slice(n * width, (n + 1) * width)
                normed[span, cols] = (v * inv * gains[s, :, cols]).astype(jnp.bfloat16)
            return carry

        lax.fori_loop(0, length // chunk, body, 0, unroll=2)

    def project(s, part, span):
        return jnp.dot(normed[span, :], wq[s, part], preferred_element_type=jnp.float32).astype(jnp.bfloat16)

    def swap(s, ref, name):
        push(ref.at[s, 0], ref.at[s, 1], arrival((name, s)), sibling)

    def block_of(n):
        return slice(n * rows, (n + 1) * rows)

    def seen_of(n):
        return [(0, n), (0, n ^ 1), (0, n ^ 2), (1, n)]

    def flag(n, side, other):
        of = 4 * (1 - half if side else half)
        return mask[zh, 4 * half + n, of + other] > 0

    def score(s, n):
        for hd in range(2):
            cols = slice(hd * HD, (hd + 1) * HD)
            query = q_ref[block_of(n), cols]
            scores, flags = [], []
            for side, other in seen_of(n):
                key = k_ref[s, side, block_of(other), cols]
                dots = lax.dot_general(query, key, (((1,), (1,)), ((), ())), preferred_element_type=jnp.float32)
                flags.append(flag(n, side, other))
                scores.append(jnp.where(flags[-1], dots * (1.0 / HD**0.5), NEG))
            top = jnp.max(functools.reduce(jnp.maximum, scores), axis=-1, keepdims=True)
            expos = [jnp.where(f, jnp.exp(v - top), 0.0) for f, v in zip(flags, scores)]
            total = jnp.sum(functools.reduce(jnp.add, expos), axis=-1, keepdims=True)
            for i, e in enumerate(expos):
                e_ref[n, hd, :, i * HD : (i + 1) * HD] = e.astype(jnp.bfloat16)
            t_ref[n, hd] = jnp.broadcast_to(total, (rows, HD))

    def mix(s, n):
        for hd in range(2):
            cols = slice(hd * HD, (hd + 1) * HD)
            summed = jnp.zeros((rows, HD), jnp.float32)
            for i, (side, other) in enumerate(seen_of(n)):
                summed = summed + jnp.dot(
                    e_ref[n, hd, :, i * HD : (i + 1) * HD], v_ref[s, side, block_of(other), cols],
                    preferred_element_type=jnp.float32,
                )
            attg[s, tile, block_of(n), cols] = (summed / t_ref[n, hd]).astype(jnp.bfloat16)

    def att_region(s, n):
        return lambda xx, yy, zz: attg.at[s, 2 * zz + xx, pl.ds(n * rows, rows), :]

    def attend(s, extra):
        arrive(k_ref.at[s, 1], arrival(("k", s)))
        for n in range(4):
            score(s, n)
        await_weights(s, VALUE)
        for g in range(2):
            span = slice(2 * g * rows, 2 * (g + 1) * rows)
            v_ref[s, 0, span, :] = project(s, VALUE, span)
        swap(s, v_ref, "v")
        arrive(v_ref.at[s, 1], arrival(("v", s)))
        spreads = []
        for n in range(4):
            mix(s, n)
            spreads.append(Spread(("a", s, n), "zx" if n % 2 else "xz", att_region(s, n)))
            spreads[-1].start()
        extra()
        await_projection(s)
        for n in range(4):
            spreads[n].stage(0)
        for n in range(4):
            spreads[n].stage(1)
            if n % 2:
                g = n // 2
                span = slice(2 * g * rows, 2 * (g + 1) * rows)
                lhs = jnp.concatenate([attg[s, i, span, :] for i in range(4)], axis=1)
                send_part[s, span, :] = jnp.dot(
                    lhs, wo[s, 1 - y], preferred_element_type=jnp.float32
                ).astype(jnp.bfloat16)
                push(
                    send_part.at[s, pl.ds(2 * g * rows, 2 * rows), :],
                    recv_part.at[s, pl.ds(2 * g * rows, 2 * rows), :],
                    arrival(("p", s, g)), partner["y"],
                )
                own_part[span, :] = jnp.dot(lhs, wo[s, y], preferred_element_type=jnp.float32)

    def total_of(s, g, before):
        span = slice(2 * g * rows, 2 * (g + 1) * rows)
        arrive(recv_part.at[s, pl.ds(2 * g * rows, 2 * rows), :], arrival(("p", s, g)))
        added = own_part[span, :] + recv_part[s, span, :].astype(jnp.float32)
        return (before(span).astype(jnp.float32) + added).astype(jnp.bfloat16)

    normalize(lambda n, span: xg[n, span, :], wide, 2, 0, 0, 4 * rows)
    every = slice(0, 4 * rows)
    await_weights(0, KEY)
    k_ref[0, 0] = project(0, KEY, every)
    swap(0, k_ref, "k")
    await_weights(0, QUERY)
    q_ref[...] = project(0, QUERY, every)
    attend(0, lambda: begin(weights[KEY], 1))
    begin(weights[QUERY], 1)
    rest_copy.wait()
    ms = [
        Spread(
            ("m", n), "zyx" if n % 2 else "zxy",
            lambda xx, yy, zz, n=n: midg.at[4 * yy + 2 * zz + xx, pl.ds(n * rows, rows), :],
        )
        for n in range(4)
    ]
    for g in range(2):
        midg[pair, 2 * g * rows : 2 * (g + 1) * rows, :] = total_of(0, g, lambda span: rest[span, :])
        for n in (2 * g, 2 * g + 1):
            ms[n].start()
    for m in ms:
        m.stage(0)
    begin(weights[VALUE] + wo_copies, 1)
    for m in ms:
        m.stage(1)
    for g in range(2):
        for n in (2 * g, 2 * g + 1):
            ms[n].stage(2)
        if g == 0:
            await_weights(1, KEY)
            await_weights(1, QUERY)
        span = slice(2 * g * rows, 2 * (g + 1) * rows)
        normalize(lambda n, at: midg[n, at, :], PAIR, 8, 1, 2 * g * rows, 2 * rows)
        k_ref[1, 0, span, :] = project(1, KEY, span)
        q_ref[span, :] = project(1, QUERY, span)
    swap(1, k_ref, "k")

    block = pl.ds(pl.multiple_of(tile * rows, rows), rows)
    outs = []
    for i in range(4):
        src, dst = midg.at[4 * y + i, block, :], out.at[zh, :, pl.ds(i * PAIR, PAIR)]
        outs.append(pltpu.make_async_copy(src, dst, loc.at[2 + i]))
        push(src, dst, arrival("mid"), dev(0, x, y, over), core == 1)

    @pl.when(core == 0)
    def _():
        for copy in outs:
            copy.start()

    attend(1, lambda: None)
    for g in range(2):
        fin[2 * g * rows : 2 * (g + 1) * rows, :] = total_of(1, g, lambda span: midg[pair, span, :])
        for n in (2 * g, 2 * g + 1):
            push(
                fin.at[pl.ds(n * rows, rows), :],
                out.at[zh, :, pl.ds(pl.multiple_of(tile * PAIR, PAIR), PAIR)],
                f_sem.at[zh], dev(1, n % 2, y, 2 * half + n // 2),
            )

    @pl.when(core == 0)
    def _():
        for copy in outs:
            copy.wait()
        arrive(out.at[1 - zh], arrival("mid"))

    @pl.when(core == 1)
    def _():
        for m in range(2):
            arrive(out.at[m], f_sem.at[m])

    for copy, when in sent:
        if when is None:
            copy.wait_send()
        else:
            pl.when(when)(copy.wait_send)


def local_cubes(feats, gain, w_qkv, w_out, block_mask):
    dma = pltpu.SemaphoreType.DMA
    bf, f32 = jnp.bfloat16, jnp.float32
    rows, wide = feats.shape[1], feats.shape[2]
    mine, whole = 4 * rows, 2 * wide
    vmem = pltpu.VMEM
    return pl.pallas_call(
        relay_kernel,
        out_shape=jax.ShapeDtypeStruct(feats.shape, bf),
        in_specs=[ANY] * 4 + [pl.BlockSpec(memory_space=pltpu.SMEM)],
        out_specs=ANY,
        scratch_shapes=[
            vmem((2, mine, wide), bf), vmem((mine, whole), bf), vmem((2, 1, whole), f32),
            vmem((2, 3, whole, PAIR), bf), vmem((2, 2, wide, PAIR), bf),
            vmem((mine, PAIR), bf), vmem((2, 2, mine, PAIR), bf), vmem((2, 2, mine, PAIR), bf),
            vmem((4, 2, rows, 4 * HD), bf), vmem((4, 2, rows, HD), f32),
            vmem((2, 4, mine, PAIR), bf), vmem((mine, PAIR), f32),
            vmem((2, mine, PAIR), bf), vmem((2, mine, PAIR), bf),
            vmem((mine, PAIR), bf), vmem((8, mine, PAIR), bf), vmem((mine, PAIR), bf),
            dma((140,)), dma((100,)), dma((2, 3)), dma((2, 2)), dma((2,)), dma((6,)),
        ],
        compiler_params=pltpu.CompilerParams(
            collective_id=0, has_side_effects=True, vmem_limit_bytes=63 * 2**20
        ),
        name="relay",
    )(feats, gain, w_qkv, w_out, block_mask)[None]


def solution(mesh):
    cubes = (mesh.shape["pipe"], mesh.shape["node"], mesh.shape["head"]) == (2, 8, 2)
    return jax.shard_map(
        local_cubes if cubes else local_any,
        mesh=mesh,
        in_specs=(
            P(None, "node", "head"),
            P("pipe", None),
            P("pipe", None, "node", "head"),
            P("pipe", "head", "node"),
            P(),
        ),
        out_specs=P("pipe", None, "node", "head"),
        check_vma=False,
    )
```

time: 180 us -> 147 us (0.82); the launches traced: 180 us -> 144 us
  Pallas kernels: 177 us -> 142 us
    pallas_call x2 -> x1, Pallas kernels: 177 us -> 142 us  [local_cubes(): pl.pallas_call(relay_kernel, out_shape=jax.ShapeDtypeStruct(feats.shape,...]
where the time goes in v1:
time: 147 us; the launch traced here: 144 us
  Pallas kernels  142 us (97%)
  local copies, waits for them, and re-layouts  1.87 us (1%)
    pallas_call x1, Pallas kernels, local_cubes(): pl.pallas_call(relay_kernel, out_shape=jax.ShapeDtypeStruct(feats.shape,...  142 us

profile of v1, /device:TPU:25, one launch (start us, length us, event | category | flops | bytes accessed | tf_op | source)
XLA Modules:
  0.0 143.7 jit_solution(17936365626736848726)
XLA Ops:
  0.0 141.8 %relay.1 = bf16[2,128,1024]{2,1,0:T(8,128)(2,1)} custom-call(bf16[2,128,1024]{2,1,0:T(8,128)(2,1)} %feats.1, f32[1,2048]{1,0:T(1,128)} %gain.1, bf16[1,3,256,1024]{3,2,1,0:T(8,128)(2,1)} %w_qkv.1, bf16[1,1024,256]{2,1,0:T(8,128)(2,1)} %w_out.1, s32[2,8,8]{2,1,0:T(8,128)} %mask.1), custom_call_target="tpu_custom_call" | custom-call | tf_op jit(solution)/shard_map/relay/pallas_call | solution.py:493
  141.8 1.9 %copy.7 = bf16[1,2,128,1024]{3,2,1,0:T(8,128)(2,1)} copy(bf16[1,2,128,1024]{3,2,1,0:T(8,128)(2,1)} %bitcast.1) | data formatting | bytes 1048576

commit v2 on v1

--- a/solution.py
+++ b/solution.py
@@ -237,10 +237,10 @@
                 spot = pl.multiple_of((2 * lax.rem(zz, 2) + xx) * PAIR, PAIR)
                 src = w_qkv.at[0, part, :, pl.ds(spot, PAIR)]
                 if d == 0 and xx is x:
-                    copies.append(pltpu.make_async_copy(src, to, w_sem.at[core, part]))
+                    copies.append(pltpu.make_async_copy(src, to, w_sem.at[core, part, zh]))
                 else:
-                    copies.append(make(src, to, w_sem.at[core, part], dev(core, xx, y, zz)))
-        return copies
+                    copies.append(make(src, to, w_sem.at[core, part, zh], dev(core, xx, y, zz)))
+        return copies[:4], copies[4:]
 
     weights = {part: weight_copies(part) for part in (KEY, QUERY, VALUE)}
     own_wo = wo.at[core, zh]
@@ -257,9 +257,19 @@
                 copy.start()
 
     def await_weights(s, part):
-        got = wq.at[s, part]
-        arrive(got, w_sem.at[s, part])
-        push(got, got, w_sem.at[s, part], sibling, core == s)
+        for b in (zh, 1 - zh):
+            got = wq.at[s, part, pl.ds(pl.multiple_of(b * 4 * depth, depth), 4 * depth), :]
+            arrive(got, w_sem.at[s, part, b])
+            push(got, got, w_sem.at[s, part, b], sibling, core == s)
+
+    later = (
+        weights[KEY][0] + weights[QUERY][0] + weights[KEY][1] + weights[VALUE][0] + weights[QUERY][1]
+        + weights[VALUE][1] + wo_copies
+    )
+
+    def drip(count):
+        begin(later[:count], 1)
+        del later[:count]
 
     def await_projection(s):
         arrive(wo.at[s, zh], o_sem.at[s, zh])
@@ -276,6 +286,7 @@
     pl.when(core == 0)(pltpu.make_async_copy(feats.at[zh], own_spot, own_key).start)
     push(gain, gains.at[core], arrival("gain"), sibling)
     keep(gain, gains.at[core], loc.at[0])
+    begin(weights[KEY][0], 0)
     arrive(own_spot, own_key)
     cut = rows // 2
     fs = [
@@ -287,13 +298,13 @@
     ]
     for f in fs:
         f.start()
-    begin(weights[KEY], 0)
+    begin(weights[QUERY][0] + weights[KEY][1], 0)
     for f in fs:
         f.stage(0)
-    begin(weights[QUERY], 0)
+    begin(weights[VALUE][0] + weights[QUERY][1], 0)
     for f in fs:
         f.stage(1)
-    begin(weights[VALUE] + wo_copies, 0)
+    begin(weights[VALUE][1] + wo_copies, 0)
     for f in fs:
         f.stage(2)
     arrive(gains.at[1 - core], arrival("gain"))
@@ -365,46 +376,51 @@
     def att_region(s, n):
         return lambda xx, yy, zz: attg.at[s, 2 * zz + xx, pl.ds(n * rows, rows), :]
 
-    def attend(s, extra):
+    def strip(n):
+        return pl.ds(n * rows, rows)
+
+    def values(s):
+        await_weights(s, VALUE)
+        v_ref[s, 0] = project(s, VALUE, slice(0, 4 * rows))
+        swap(s, v_ref, "v")
+
+    def total_of(s, n, before):
+        arrive(recv_part.at[s, strip(n), :], arrival(("p", s, n)))
+        added = own_part[block_of(n), :] + recv_part[s, block_of(n), :].astype(jnp.float32)
+        return (before[block_of(n), :].astype(jnp.float32) + added).astype(jnp.bfloat16)
+
+    def attend(s, combine):
+        if s == 1:
+            values(s)
         arrive(k_ref.at[s, 1], arrival(("k", s)))
         for n in range(4):
             score(s, n)
-        await_weights(s, VALUE)
-        for g in range(2):
-            span = slice(2 * g * rows, 2 * (g + 1) * rows)
-            v_ref[s, 0, span, :] = project(s, VALUE, span)
-        swap(s, v_ref, "v")
+        if s == 0:
+            values(s)
         arrive(v_ref.at[s, 1], arrival(("v", s)))
         spreads = []
         for n in range(4):
             mix(s, n)
             spreads.append(Spread(("a", s, n), "zx" if n % 2 else "xz", att_region(s, n)))
             spreads[-1].start()
-        extra()
+        drip(2)
         await_projection(s)
         for n in range(4):
             spreads[n].stage(0)
+            drip(1)
         for n in range(4):
             spreads[n].stage(1)
-            if n % 2:
-                g = n // 2
-                span = slice(2 * g * rows, 2 * (g + 1) * rows)
-                lhs = jnp.concatenate([attg[s, i, span, :] for i in range(4)], axis=1)
-                send_part[s, span, :] = jnp.dot(
-                    lhs, wo[s, 1 - y], preferred_element_type=jnp.float32
-                ).astype(jnp.bfloat16)
-                push(
-                    send_part.at[s, pl.ds(2 * g * rows, 2 * rows), :],
-                    recv_part.at[s, pl.ds(2 * g * rows, 2 * rows), :],
-                    arrival(("p", s, g)), partner["y"],
-                )
-                own_part[span, :] = jnp.dot(lhs, wo[s, y], preferred_element_type=jnp.float32)
-
-    def total_of(s, g, before):
-        span = slice(2 * g * rows, 2 * (g + 1) * rows)
-        arrive(recv_part.at[s, pl.ds(2 * g * rows, 2 * rows), :], arrival(("p", s, g)))
-        added = own_part[span, :] + recv_part[s, span, :].astype(jnp.float32)
-        return (before(span).astype(jnp.float32) + added).astype(jnp.bfloat16)
+            span = block_of(n)
+            lhs = jnp.concatenate([attg[s, i, span, :] for i in range(4)], axis=1)
+            send_part[s, span, :] = jnp.dot(lhs, wo[s, 1 - y], preferred_element_type=jnp.float32).astype(jnp.bfloat16)
+            push(
+                send_part.at[s, strip(n), :], recv_part.at[s, strip(n), :], arrival(("p", s, n)), partner["y"]
+            )
+            own_part[span, :] = jnp.dot(lhs, wo[s, y], preferred_element_type=jnp.float32)
+            drip(1)
+            if n:
+                combine(n - 1)
+        combine(3)
 
     normalize(lambda n, span: xg[n, span, :], wide, 2, 0, 0, 4 * rows)
     every = slice(0, 4 * rows)
@@ -413,35 +429,35 @@
     swap(0, k_ref, "k")
     await_weights(0, QUERY)
     q_ref[...] = project(0, QUERY, every)
-    attend(0, lambda: begin(weights[KEY], 1))
-    begin(weights[QUERY], 1)
     rest_copy.wait()
     ms = [
         Spread(
-            ("m", n), "zyx" if n % 2 else "zxy",
-            lambda xx, yy, zz, n=n: midg.at[4 * yy + 2 * zz + xx, pl.ds(n * rows, rows), :],
+            ("m", n), "zyx" if n == 1 else "zxy",
+            lambda xx, yy, zz, n=n: midg.at[4 * yy + 2 * zz + xx, strip(n), :],
         )
         for n in range(4)
     ]
-    for g in range(2):
-        midg[pair, 2 * g * rows : 2 * (g + 1) * rows, :] = total_of(0, g, lambda span: rest[span, :])
-        for n in (2 * g, 2 * g + 1):
-            ms[n].start()
+
+    def middle(n):
+        midg[pair, block_of(n), :] = total_of(0, n, rest)
+        ms[n].start()
+        drip(1)
+
+    attend(0, middle)
     for m in ms:
         m.stage(0)
-    begin(weights[VALUE] + wo_copies, 1)
+        drip(1)
     for m in ms:
         m.stage(1)
-    for g in range(2):
-        for n in (2 * g, 2 * g + 1):
-            ms[n].stage(2)
-        if g == 0:
-            await_weights(1, KEY)
-            await_weights(1, QUERY)
-        span = slice(2 * g * rows, 2 * (g + 1) * rows)
-        normalize(lambda n, at: midg[n, at, :], PAIR, 8, 1, 2 * g * rows, 2 * rows)
-        k_ref[1, 0, span, :] = project(1, KEY, span)
-        q_ref[span, :] = project(1, QUERY, span)
+        drip(2)
+    drip(len(later))
+    await_weights(1, KEY)
+    await_weights(1, QUERY)
+    for n in range(4):
+        ms[n].stage(2)
+        normalize(lambda i, at: midg[i, at, :], PAIR, 8, 1, n * rows, rows)
+        k_ref[1, 0, block_of(n), :] = project(1, KEY, block_of(n))
+        q_ref[block_of(n), :] = project(1, QUERY, block_of(n))
     swap(1, k_ref, "k")
 
     block = pl.ds(pl.multiple_of(tile * rows, rows), rows)
@@ -456,15 +472,14 @@
         for copy in outs:
             copy.start()
 
-    attend(1, lambda: None)
-    for g in range(2):
-        fin[2 * g * rows : 2 * (g + 1) * rows, :] = total_of(1, g, lambda span: midg[pair, span, :])
-        for n in (2 * g, 2 * g + 1):
-            push(
-                fin.at[pl.ds(n * rows, rows), :],
-                out.at[zh, :, pl.ds(pl.multiple_of(tile * PAIR, PAIR), PAIR)],
-                f_sem.at[zh], dev(1, n % 2, y, 2 * half + n // 2),
-            )
+    def last(n):
+        fin[block_of(n), :] = total_of(1, n, midg.at[pair])
+        push(
+            fin.at[strip(n), :], out.at[zh, :, pl.ds(pl.multiple_of(tile * PAIR, PAIR), PAIR)],
+            f_sem.at[zh], dev(1, n % 2, y, 2 * half + n // 2),
+        )
+
+    attend(1, last)
 
     @pl.when(core == 0)
     def _():
@@ -503,7 +518,7 @@
             vmem((2, 4, mine, PAIR), bf), vmem((mine, PAIR), f32),
             vmem((2, mine, PAIR), bf), vmem((2, mine, PAIR), bf),
             vmem((mine, PAIR), bf), vmem((8, mine, PAIR), bf), vmem((mine, PAIR), bf),
-            dma((140,)), dma((100,)), dma((2, 3)), dma((2, 2)), dma((2,)), dma((6,)),
+            dma((160,)), dma((110,)), dma((2, 3, 2)), dma((2, 2)), dma((2,)), dma((6,)),
         ],
         compiler_params=pltpu.CompilerParams(
             collective_id=0, has_side_effects=True, vmem_limit_bytes=63 * 2**20

time: 147 us -> 135 us (0.918); the launches traced: 144 us -> 133 us
  Pallas kernels: 142 us -> 131 us
    pallas_call x1, Pallas kernels: 142 us -> 131 us  [local_cubes(): pl.pallas_call(relay_kernel, out_shape=jax.ShapeDtypeStruct(feats.shape,...]
where the time goes in v2:
time: 135 us; the launch traced here: 133 us
  Pallas kernels  131 us (97%)
  local copies, waits for them, and re-layouts  1.87 us (1%)
    pallas_call x1, Pallas kernels, local_cubes(): pl.pallas_call(relay_kernel, out_shape=jax.ShapeDtypeStruct(feats.shape,...  131 us

profile of v2, /device:TPU:25, one launch (start us, length us, event | category | flops | bytes accessed | tf_op | source)
XLA Modules:
  0.0 133.2 jit_solution(18081129151978988533)
XLA Ops:
  0.0 131.4 %relay.1 = bf16[2,128,1024]{2,1,0:T(8,128)(2,1)} custom-call(bf16[2,128,1024]{2,1,0:T(8,128)(2,1)} %feats.1, f32[1,2048]{1,0:T(1,128)} %gain.1, bf16[1,3,256,1024]{3,2,1,0:T(8,128)(2,1)} %w_qkv.1, bf16[1,1024,256]{2,1,0:T(8,128)(2,1)} %w_out.1, s32[2,8,8]{2,1,0:T(8,128)} %mask.1), custom_call_target="tpu_custom_call" | custom-call | tf_op jit(solution)/shard_map/relay/pallas_call | solution.py:508
  131.4 1.9 %copy.7 = bf16[1,2,128,1024]{3,2,1,0:T(8,128)(2,1)} copy(bf16[1,2,128,1024]{3,2,1,0:T(8,128)(2,1)} %bitcast.1) | data formatting | bytes 1048576

commit v3 on v2

--- a/solution.py
+++ b/solution.py
@@ -230,7 +230,7 @@
 
     def weight_copies(part):
         copies = []
-        to = wq.at[core, part, pl.ds(pl.multiple_of((2 * z + x) * depth, depth), depth), :]
+        to = wq.at[core, part, zh, pl.ds(pl.multiple_of(tile * depth, depth), depth), :]
         for d in (2, 3, 1, 0):
             for xx in (1 - x, x):
                 zz = z_apart(z, d)
@@ -256,14 +256,13 @@
             for copy in copies:
                 copy.start()
 
-    def await_weights(s, part):
-        for b in (zh, 1 - zh):
-            got = wq.at[s, part, pl.ds(pl.multiple_of(b * 4 * depth, depth), 4 * depth), :]
-            arrive(got, w_sem.at[s, part, b])
-            push(got, got, w_sem.at[s, part, b], sibling, core == s)
+    def await_weights(s, part, b):
+        got = wq.at[s, part, b]
+        arrive(got, w_sem.at[s, part, b])
+        push(got, got, w_sem.at[s, part, b], sibling, core == s)
 
     later = (
-        weights[KEY][0] + weights[QUERY][0] + weights[KEY][1] + weights[VALUE][0] + weights[QUERY][1]
+        weights[KEY][0] + weights[QUERY][0] + weights[KEY][1] + weights[QUERY][1] + weights[VALUE][0]
         + weights[VALUE][1] + wo_copies
     )
 
@@ -324,13 +323,20 @@
             inv = lax.rsqrt(squares * (1.0 / (width * count)) + EPS)
             for n, v in enumerate(xs):
                 cols = slice(n * width, (n + 1) * width)
-                normed[span, cols] = (v * inv * gains[s, :, cols]).astype(jnp.bfloat16)
+                b, at = divmod(n * width, wide)
+                normed[b, span, at : at + width] = (v * inv * gains[s, :, cols]).astype(jnp.bfloat16)
             return carry
 
         lax.fori_loop(0, length // chunk, body, 0, unroll=2)
 
-    def project(s, part, span):
-        return jnp.dot(normed[span, :], wq[s, part], preferred_element_type=jnp.float32).astype(jnp.bfloat16)
+    def project(s, part, span, wait=True):
+        total = None
+        for b in (zh, 1 - zh):
+            if wait:
+                await_weights(s, part, b)
+            term = jnp.dot(normed[b, span, :], wq[s, part, b], preferred_element_type=jnp.float32)
+            total = term if total is None else total + term
+        return total.astype(jnp.bfloat16)
 
     def swap(s, ref, name):
         push(ref.at[s, 0], ref.at[s, 1], arrival((name, s)), sibling)
@@ -380,7 +386,6 @@
         return pl.ds(n * rows, rows)
 
     def values(s):
-        await_weights(s, VALUE)
         v_ref[s, 0] = project(s, VALUE, slice(0, 4 * rows))
         swap(s, v_ref, "v")
 
@@ -389,7 +394,7 @@
         added = own_part[block_of(n), :] + recv_part[s, block_of(n), :].astype(jnp.float32)
         return (before[block_of(n), :].astype(jnp.float32) + added).astype(jnp.bfloat16)
 
-    def attend(s, combine):
+    def attend(s, combine, between):
         if s == 1:
             values(s)
         arrive(k_ref.at[s, 1], arrival(("k", s)))
@@ -403,11 +408,12 @@
             mix(s, n)
             spreads.append(Spread(("a", s, n), "zx" if n % 2 else "xz", att_region(s, n)))
             spreads[-1].start()
-        drip(2)
+        drip(1)
         await_projection(s)
         for n in range(4):
             spreads[n].stage(0)
             drip(1)
+        between()
         for n in range(4):
             spreads[n].stage(1)
             span = block_of(n)
@@ -424,10 +430,8 @@
 
     normalize(lambda n, span: xg[n, span, :], wide, 2, 0, 0, 4 * rows)
     every = slice(0, 4 * rows)
-    await_weights(0, KEY)
     k_ref[0, 0] = project(0, KEY, every)
     swap(0, k_ref, "k")
-    await_weights(0, QUERY)
     q_ref[...] = project(0, QUERY, every)
     rest_copy.wait()
     ms = [
@@ -441,9 +445,9 @@
     def middle(n):
         midg[pair, block_of(n), :] = total_of(0, n, rest)
         ms[n].start()
-        drip(1)
-
-    attend(0, middle)
+        drip(2)
+
+    attend(0, middle, lambda: None)
     for m in ms:
         m.stage(0)
         drip(1)
@@ -451,26 +455,29 @@
         m.stage(1)
         drip(2)
     drip(len(later))
-    await_weights(1, KEY)
-    await_weights(1, QUERY)
+    for part in (KEY, QUERY):
+        for b in (zh, 1 - zh):
+            await_weights(1, part, b)
     for n in range(4):
         ms[n].stage(2)
         normalize(lambda i, at: midg[i, at, :], PAIR, 8, 1, n * rows, rows)
-        k_ref[1, 0, block_of(n), :] = project(1, KEY, block_of(n))
-        q_ref[block_of(n), :] = project(1, QUERY, block_of(n))
+        k_ref[1, 0, block_of(n), :] = project(1, KEY, block_of(n), False)
+        q_ref[block_of(n), :] = project(1, QUERY, block_of(n), False)
     swap(1, k_ref, "k")
 
     block = pl.ds(pl.multiple_of(tile * rows, rows), rows)
     outs = []
-    for i in range(4):
-        src, dst = midg.at[4 * y + i, block, :], out.at[zh, :, pl.ds(i * PAIR, PAIR)]
-        outs.append(pltpu.make_async_copy(src, dst, loc.at[2 + i]))
-        push(src, dst, arrival("mid"), dev(0, x, y, over), core == 1)
-
-    @pl.when(core == 0)
-    def _():
-        for copy in outs:
-            copy.start()
+
+    def first_output():
+        for i in range(4):
+            src, dst = midg.at[4 * y + i, block, :], out.at[zh, :, pl.ds(i * PAIR, PAIR)]
+            outs.append(pltpu.make_async_copy(src, dst, loc.at[2 + i]))
+            push(src, dst, arrival("mid"), dev(0, x, y, over), core == 1)
+
+        @pl.when(core == 0)
+        def _():
+            for copy in outs:
+                copy.start()
 
     def last(n):
         fin[block_of(n), :] = total_of(1, n, midg.at[pair])
@@ -479,7 +486,7 @@
             f_sem.at[zh], dev(1, n % 2, y, 2 * half + n // 2),
         )
 
-    attend(1, last)
+    attend(1, last, first_output)
 
     @pl.when(core == 0)
     def _():
@@ -511,8 +518,8 @@
         in_specs=[ANY] * 4 + [pl.BlockSpec(memory_space=pltpu.SMEM)],
         out_specs=ANY,
         scratch_shapes=[
-            vmem((2, mine, wide), bf), vmem((mine, whole), bf), vmem((2, 1, whole), f32),
-            vmem((2, 3, whole, PAIR), bf), vmem((2, 2, wide, PAIR), bf),
+            vmem((2, mine, wide), bf), vmem((2, mine, wide), bf), vmem((2, 1, whole), f32),
+            vmem((2, 3, 2, wide, PAIR), bf), vmem((2, 2, wide, PAIR), bf),
             vmem((mine, PAIR), bf), vmem((2, 2, mine, PAIR), bf), vmem((2, 2, mine, PAIR), bf),
             vmem((4, 2, rows, 4 * HD), bf), vmem((4, 2, rows, HD), f32),
             vmem((2, 4, mine, PAIR), bf), vmem((mine, PAIR), f32),

time: 135 us -> 138 us (1.022)
  Pallas kernels: 131 us -> 135 us
    pallas_call x1, Pallas kernels: 131 us -> 135 us  [local_cubes(): pl.pallas_call(relay_kernel, out_shape=jax.ShapeDtypeStruct(feats.shape,...]
where the time goes in v3:
time: 138 us; the launch traced here: 137 us
  Pallas kernels  135 us (98%)
  local copies, waits for them, and re-layouts  1.87 us (1%)
    pallas_call x1, Pallas kernels, local_cubes(): pl.pallas_call(relay_kernel, out_shape=jax.ShapeDtypeStruct(feats.shape,...  135 us

profile of v3, /device:TPU:25, one launch (start us, length us, event | category | flops | bytes accessed | tf_op | source)
XLA Modules:
  0.0 136.7 jit_solution(18391089049293661489)
XLA Ops:
  0.0 134.9 %relay.1 = bf16[2,128,1024]{2,1,0:T(8,128)(2,1)} custom-call(bf16[2,128,1024]{2,1,0:T(8,128)(2,1)} %feats.1, f32[1,2048]{1,0:T(1,128)} %gain.1, bf16[1,3,256,1024]{3,2,1,0:T(8,128)(2,1)} %w_qkv.1, bf16[1,1024,256]{2,1,0:T(8,128)(2,1)} %w_out.1, s32[2,8,8]{2,1,0:T(8,128)} %mask.1), custom_call_target="tpu_custom_call" | custom-call | tf_op jit(solution)/shard_map/relay/pallas_call | solution.py:515
  134.9 1.9 %copy.7 = bf16[1,2,128,1024]{3,2,1,0:T(8,128)(2,1)} copy(bf16[1,2,128,1024]{3,2,1,0:T(8,128)(2,1)} %bitcast.1) | data formatting | bytes 1048576

commit v4 on v3

--- a/solution.py
+++ b/solution.py
@@ -394,7 +394,7 @@
         added = own_part[block_of(n), :] + recv_part[s, block_of(n), :].astype(jnp.float32)
         return (before[block_of(n), :].astype(jnp.float32) + added).astype(jnp.bfloat16)
 
-    def attend(s, combine, between):
+    def attend(s, combine):
         if s == 1:
             values(s)
         arrive(k_ref.at[s, 1], arrival(("k", s)))
@@ -408,12 +408,11 @@
             mix(s, n)
             spreads.append(Spread(("a", s, n), "zx" if n % 2 else "xz", att_region(s, n)))
             spreads[-1].start()
-        drip(1)
+        drip(2)
         await_projection(s)
         for n in range(4):
             spreads[n].stage(0)
             drip(1)
-        between()
         for n in range(4):
             spreads[n].stage(1)
             span = block_of(n)
@@ -445,9 +444,9 @@
     def middle(n):
         midg[pair, block_of(n), :] = total_of(0, n, rest)
         ms[n].start()
-        drip(2)
-
-    attend(0, middle, lambda: None)
+        drip(1)
+
+    attend(0, middle)
     for m in ms:
         m.stage(0)
         drip(1)
@@ -486,7 +485,8 @@
             f_sem.at[zh], dev(1, n % 2, y, 2 * half + n // 2),
         )
 
-    attend(1, last, first_output)
+    first_output()
+    attend(1, last)
 
     @pl.when(core == 0)
     def _():

time: 138 us -> 139 us (level); the launches traced: 137 us -> 136 us
  no operation moved by 1% of the time
where the time goes in v4:
time: 139 us; the launch traced here: 136 us
  Pallas kernels  134 us (96%)
  local copies, waits for them, and re-layouts  1.87 us (1%)
    pallas_call x1, Pallas kernels, local_cubes(): pl.pallas_call(relay_kernel, out_shape=jax.ShapeDtypeStruct(feats.shape,...  134 us

profile of v4, /device:TPU:25, one launch (start us, length us, event | category | flops | bytes accessed | tf_op | source)
XLA Modules:
  0.0 136.0 jit_solution(7349859395583952803)
XLA Ops:
  0.0 134.1 %relay.1 = bf16[2,128,1024]{2,1,0:T(8,128)(2,1)} custom-call(bf16[2,128,1024]{2,1,0:T(8,128)(2,1)} %feats.1, f32[1,2048]{1,0:T(1,128)} %gain.1, bf16[1,3,256,1024]{3,2,1,0:T(8,128)(2,1)} %w_qkv.1, bf16[1,1024,256]{2,1,0:T(8,128)(2,1)} %w_out.1, s32[2,8,8]{2,1,0:T(8,128)} %mask.1), custom_call_target="tpu_custom_call" | custom-call | tf_op jit(solution)/shard_map/relay/pallas_call | solution.py:515
  134.2 1.9 %copy.7 = bf16[1,2,128,1024]{3,2,1,0:T(8,128)(2,1)} copy(bf16[1,2,128,1024]{3,2,1,0:T(8,128)(2,1)} %bitcast.1) | data formatting | bytes 1048576
